TPU v7x, 32 devices: a whole 2x2x4 slice. The times are simulated.
32 devices in a mesh: dp: 2 (over x), slot: 4 (over y, core), hid: 4 (over z).
Axes of the slice: x: 2, y: 2, z: 4, core: 2. Of those that a mesh axis runs over, the one named last changes fastest.
Arguments:
- master_weights: float32 [8, 3, 768, 2048], P('slot', None, 'hid', 'dp'), may hold values from -0.125 to 0.125
- first_moment: float32 [8, 3, 768, 2048], P('slot', None, 'hid', 'dp'), may hold values from -6 to 6
- second_moment: float32 [8, 3, 768, 2048], P('slot', None, 'hid', 'dp'), may hold values from 1 to 100
- tokens_one: bfloat16 [2048, 2048], P('dp'), may hold values from -6 to 6
- grad_out: bfloat16 [2048, 2048], P('dp'), may hold values from -6 to 6
- route_one: int32 [2048, 2], P('dp'), may hold values from 0 to 7, all different within a row
- prob_one: float32 [2048, 2], P('dp'), may hold values from 0.05 to 0.6
- tokens_two: bfloat16 [2048, 2048], P('dp'), may hold values from -6 to 6
- route_two: int32 [2048, 2], P('dp'), may hold values from 0 to 7, all different within a row
- prob_two: float32 [2048, 2], P('dp'), may hold values from 0.05 to 0.6
- old_order: int32 [8], replicated, may hold values from 0 to 7, each once
- new_order: int32 [8], replicated, may hold values from 0 to 7, each once
Outputs:
- moved_master: float32 [8, 3, 768, 2048], P('slot', None, 'hid', 'dp')
- moved_first: float32 [8, 3, 768, 2048], P('slot', None, 'hid', 'dp')
- moved_second: float32 [8, 3, 768, 2048], P('slot', None, 'hid', 'dp')
- next_output: bfloat16 [2048, 2048], P('dp', ('slot', 'hid'))
Inputs may be any that keep to these rules, and one draw needn't show every extreme that they name: `old_order`: lists each of the 8 experts once. `new_order`: lists each of the 8 experts once. `route_one`: each row names 2 different experts. `route_two`: each row names 2 different experts.
All inputs are finite; a program needn't handle non-finite values.
Results may differ from a plain program's by a relative error of at most 0.017.
Values may be sent and summed in bfloat16 or wider, within the bound.
A program may use at most 192 MiB of HBM per device.

v0:
```python
import jax
import jax.numpy as jnp
from jax import lax
from jax.sharding import PartitionSpec as P

learn_rate = 0.001
beta_one = 0.9
beta_two = 0.95
epsilon = 1e-08
decay_rate = 0.1


def rows_by(left, right):
    return lax.dot_general(
        left, right, (((1,), (1,)), ((), ())), preferred_element_type=jnp.float32
    )


def cols_by(left, right):
    return lax.dot_general(
        left, right, (((0,), (0,)), ((), ())), preferred_element_type=jnp.float32
    )


def expert_parts(tokens, grad_out, scaling, weights):
    gate_proj = rows_by(tokens, weights[0])
    up_proj = rows_by(tokens, weights[1])
    logistic = jax.nn.sigmoid(gate_proj)
    swish_gate = gate_proj * logistic
    activated = (swish_gate * up_proj).astype(jnp.bfloat16)
    scaled_grad = (scaling[:, None] * grad_out.astype(jnp.float32)).astype(jnp.bfloat16)
    d_activated = rows_by(scaled_grad, weights[2])
    d_gate = (d_activated * up_proj * logistic * (1.0 + gate_proj * (1.0 - logistic))).astype(
        jnp.bfloat16
    )
    d_up = (d_activated * swish_gate).astype(jnp.bfloat16)
    return (d_gate, d_up, activated, scaled_grad)


def expert_out(tokens, scaling, weights):
    gate_proj = rows_by(tokens, weights[0])
    up_proj = rows_by(tokens, weights[1])
    mixed = (scaling[:, None] * gate_proj * jax.nn.sigmoid(gate_proj) * up_proj).astype(
        jnp.bfloat16
    )
    return jnp.dot(mixed, weights[2], preferred_element_type=jnp.float32)


def adamw_update(master, moment_a, moment_b, grad_sum):
    new_a = beta_one * moment_a + (1.0 - beta_one) * grad_sum
    new_b = beta_two * moment_b + (1.0 - beta_two) * grad_sum * grad_sum
    fixed_a = new_a / (1.0 - beta_one**10)
    fixed_b = new_b / (1.0 - beta_two**10)
    new_master = master - learn_rate * (
        fixed_a / (jnp.sqrt(fixed_b) + epsilon) + decay_rate * master
    )
    return (new_master, new_a, new_b)


def coefficients(routes, probs, expert_ids):
    matches = routes[:, :, None] == expert_ids[None, None, :]
    return jnp.sum(jnp.where(matches, probs[:, :, None], 0.0), axis=1)


def per_device(
    master_weights,
    first_moment,
    second_moment,
    tokens_one,
    grad_out,
    route_one,
    prob_one,
    tokens_two,
    route_two,
    prob_two,
    old_order,
    new_order,
):
    local_count = master_weights.shape[0]
    slot_index = lax.axis_index("slot")
    offset = slot_index * local_count
    held_ids = lax.dynamic_slice_in_dim(old_order, offset, local_count)
    shard_weights = master_weights.astype(jnp.bfloat16)
    full_weights = lax.all_gather(shard_weights, "dp", axis=3, tiled=True)
    scaling_one = coefficients(route_one, prob_one, held_ids)
    parts = [
        expert_parts(tokens_one, grad_out, scaling_one[:, expert], full_weights[expert])
        for expert in range(local_count)
    ]
    gradients = jnp.stack(
        [
            jnp.stack(
                [
                    cols_by(part[0], tokens_one),
                    cols_by(part[1], tokens_one),
                    cols_by(part[2], part[3]),
                ]
            )
            for part in parts
        ]
    )
    owned_grads = lax.psum_scatter(
        gradients.astype(jnp.bfloat16), "dp", scatter_dimension=3, tiled=True
    ).astype(jnp.float32)
    new_master, new_a, new_b = adamw_update(
        master_weights, first_moment, second_moment, owned_grads
    )
    positions = jnp.arange(old_order.shape[0], dtype=jnp.int32)
    source = jnp.sum(
        jnp.where(old_order[None, :] == new_order[:, None], positions[None, :], 0), axis=1
    )
    gathered_states = (
        lax.all_gather(new_master, "slot", axis=0, tiled=True),
        lax.all_gather(new_a, "slot", axis=0, tiled=True),
        lax.all_gather(new_b, "slot", axis=0, tiled=True),
    )
    wanted = lax.dynamic_slice_in_dim(source, offset, local_count)
    moved_states = tuple((jnp.take(state_block, wanted, axis=0) for state_block in gathered_states))
    moved_master, moved_first, moved_second = moved_states
    next_shard = new_master.astype(jnp.bfloat16)
    next_full = lax.all_gather(next_shard, "dp", axis=3, tiled=True)
    scaling_two = coefficients(route_two, prob_two, held_ids)
    partial_value = expert_out(tokens_two, scaling_two[:, 0], next_full[0])
    expert = 1
    partial_value = partial_value + expert_out(
        tokens_two, scaling_two[:, expert], next_full[expert]
    )
    mixed_out = lax.psum_scatter(
        partial_value, ("slot", "hid"), scatter_dimension=1, tiled=True
    ).astype(jnp.bfloat16)
    return (moved_master, moved_first, moved_second, mixed_out)


def solution(mesh):
    in_specs = (
        P("slot", None, "hid", "dp"),
        P("slot", None, "hid", "dp"),
        P("slot", None, "hid", "dp"),
        P("dp", None),
        P("dp", None),
        P("dp", None),
        P("dp", None),
        P("dp", None),
        P("dp", None),
        P("dp", None),
        P(),
        P(),
    )
    out_specs = (
        P("slot", None, "hid", "dp"),
        P("slot", None, "hid", "dp"),
        P("slot", None, "hid", "dp"),
        P("dp", ("slot", "hid")),
    )
    return jax.shard_map(
        per_device, mesh=mesh, in_specs=in_specs, out_specs=out_specs, check_vma=False
    )
```

profile of v0, /device:TPU:0, one launch (start us, length us, event | category | flops | bytes accessed | tf_op | source)
XLA Modules:
  0.0 761.6 jit_solution(9084671307208111710)
XLA Ops:
  7.3 4.1 convert_element_type.49
  11.7 65.2 %all-gather.6.cloned.1.call-done = bf16[2,3,192,2048]{3,2,1,0:T(8,128)(2,1)} async-done(((bf16[2,3,192,1024]{3,2,1,0:T(8,128)(2,1)}), bf16[2,3,192,2048]{3,2,1,0:T(8,128)(2,1)}) %all-gather.6.cloned.1.call-update) | async-done | bytes 4718608 | tf_op jit(solution)/shard_map/all_gather | solution.py:84
  76.9 4.1 fusion.23
  81.0 4.0 fusion.14
  86.1 1.5 fusion.24
  92.7 1.6 fusion.11
  95.4 1.5 fusion.22
  100.1 2.6 pad_maximum_fusion
  102.8 60.2 %reduce-scatter.3.cloned.1.call-done = bf16[2,3,192,1024]{3,2,1,0:T(8,128)(2,1)} async-done(((bf16[2,3,192,2048]{3,2,1,0:T(8,128)(2,1)}), bf16[2,3,192,1024]{3,2,1,0:T(8,128)(2,1)}) %reduce-scatter.3.cloned.1.call-update) | async-done | bytes 2359312 | tf_op jit(solution)/shard_map/reduce_scatter | solution.py:102
  163.0 11.4 %fusion.59 = (bf16[2,3,192,1024]{3,2,1,0:T(8,128)(2,1)}, f32[2,3,192,1024]{3,2,1,0:T(8,128)}, f32[2,3,192,1024]{3,2,1,0:T(8,128)}, f32[2,3,192,1024]{3,2,1,0:T(8,128)}) fusion(f32[2,3,192,1024]{3,2,1,0:T(8,128)} %param.14, bf16[2,3,192,1024]{3,2,1,0:T(8,128)(2,1)} %reduce-scatter.3.cloned.1.call-done, f32[2,3,192,1024]{3,2,1,0:T(8,128)} %param.15, ...), kind=kLoop, calls=%fused_computation.100 | loop fusion | flops 20054016 | bytes 33030144 | tf_op jit(solution)/shard_map/convert_element_type | solution.py:120
  174.4 62.7 %all-gather.14.cloned.1.call-done = bf16[2,3,192,2048]{3,2,1,0:T(8,128)(2,1)} async-done(((bf16[2,3,192,1024]{3,2,1,0:T(8,128)(2,1)}), bf16[2,3,192,2048]{3,2,1,0:T(8,128)(2,1)}) %all-gather.14.cloned.1.call-update) | async-done | bytes 4718608 | tf_op jit(solution)/shard_map/all_gather | solution.py:121
  237.1 4.1 fusion.20
  241.3 2.7 fusion.19
  243.9 8.7 %fusion.17 = f32[1024,2048]{1,0:T(8,128)} fusion(bf16[1024,2048]{1,0:T(8,128)(2,1)} %param.21, bf16[2,3,192,2048]{3,2,1,0:T(8,128)(2,1)} %all-gather.14.cloned.1.call-done, f32[192,1024]{1,0:T(8,128)S(1)} %fusion.20, f32[1024]{0:T(1024)S(1)} %bitcast.71), kind=kOutput, calls=%fused_computation.36 | convolution fusion | flops 1611988992 | bytes 14946304 | tf_op jit(solution)/shard_map/dot_general | solution.py:46
  252.6 11.2 %convolution_add_fusion = f32[1024,2048]{1,0:T(8,128)} fusion(f32[1024,2048]{1,0:T(8,128)} %fusion.17, bf16[1024,2048]{1,0:T(8,128)(2,1)} %param.21, bf16[2,3,192,2048]{3,2,1,0:T(8,128)(2,1)} %all-gather.14.cloned.1.call-done, f32[192,1024]{1,0:T(8,128)S(1)} %fusion.19, f32[1024]{0:T(1024)S(1)} %bitcast.70), kind=kOutput, calls=%fused_computation.13 | convolution fusion | flops 1614086144 | bytes 23334912 | tf_op jit(solution)/shard_map/dot_general | solution.py:46
  266.1 101.5 %reduce-scatter.5.cloned.1.call-done = f32[1024,128]{1,0:T(8,128)} async-done(((f32[1024,2048]{1,0:T(8,128)}), f32[1024,128]{1,0:T(8,128)}) %reduce-scatter.5.cloned.1.call-update) | async-done | bytes 524304 | tf_op jit(solution)/shard_map/reduce_scatter | solution.py:128
  367.6 1.8 convert_element_type.61
  369.4 119.9 %all-gather.8.cloned.1.call-done = f32[8,3,192,1024]{3,2,1,0:T(8,128)} async-done(((f32[2,3,192,1024]{3,2,1,0:T(8,128)}), f32[8,3,192,1024]{3,2,1,0:T(8,128)}) %all-gather.8.cloned.1.call-update) | async-done | bytes 18874384 | tf_op jit(solution)/shard_map/all_gather | solution.py:113
  489.3 9.7 %gather_fusion = f32[2,3,192,1024]{3,2,1,0:T(8,128)} fusion(f32[8,3,192,1024]{3,2,1,0:T(8,128)} %all-gather.8.cloned.1.call-done, s32[1024]{0:T(1024)S(1)} %pad_clamp_fusion), kind=kCustom, calls=%fused_computation.clone | custom fusion | bytes 9437192 | tf_op jit(solution)/shard_map/jit(_take)/gather | solution.py:118
  499.0 112.4 %all-gather.10.cloned.1.call-done = f32[8,3,192,1024]{3,2,1,0:T(8,128)} async-done(((f32[2,3,192,1024]{3,2,1,0:T(8,128)}), f32[8,3,192,1024]{3,2,1,0:T(8,128)}) %all-gather.10.cloned.1.call-update) | async-done | bytes 18874384 | tf_op jit(solution)/shard_map/all_gather | solution.py:114
  611.3 9.7 %gather_fusion.1 = f32[2,3,192,1024]{3,2,1,0:T(8,128)} fusion(f32[8,3,192,1024]{3,2,1,0:T(8,128)} %all-gather.10.cloned.1.call-done, s32[1024]{0:T(1024)S(1)} %pad_clamp_fusion), kind=kCustom, calls=%fused_computation.1.clone | custom fusion | bytes 9437192 | tf_op jit(solution)/shard_map/jit(_take)/gather | solution.py:118
  621.0 112.5 %all-gather.12.cloned.1.call-done = f32[8,3,192,1024]{3,2,1,0:T(8,128)} async-done(((f32[2,3,192,1024]{3,2,1,0:T(8,128)}), f32[8,3,192,1024]{3,2,1,0:T(8,128)}) %all-gather.12.cloned.1.call-update) | async-done | bytes 18874384 | tf_op jit(solution)/shard_map/all_gather | solution.py:115
  733.5 9.4 %gather_fusion.2 = f32[2,3,192,1024]{3,2,1,0:T(8,128)} fusion(f32[8,3,192,1024]{3,2,1,0:T(8,128)} %all-gather.12.cloned.1.call-done, s32[1024]{0:T(1024)S(1)} %pad_clamp_fusion), kind=kCustom, calls=%fused_computation.2.clone | custom fusion | bytes 9437192 | tf_op jit(solution)/shard_map/jit(_take)/gather | solution.py:118
  742.9 11.9 %broadcast_select_fusion = (f32[2,3,192,1024]{3,2,1,0:T(8,128)}, f32[2,3,192,1024]{3,2,1,0:T(8,128)}, f32[2,3,192,1024]{3,2,1,0:T(8,128)}) fusion(f32[2,3,192,1024]{3,2,1,0:T(8,128)} %gather_fusion.2, pred[2]{0:T(512)(128)(4,1)S(1)} %get-tuple-element.11, f32[2,3,192,1024]{3,2,1,0:T(8,128)} %gather_fusion.1, f32[2,3,192,1024]{3,2,1,0:T(8,128)} %gather_fusion), kind=kLoop, calls=%fused_computation.28 | loop fusion | flops 3538944 | bytes 28311554 | tf_op jit(solution)/shard_map/jit(_take)/select_n | solution.py:118
  (49 shorter events, 12.8 us)
Async XLA Ops:
  7.2 4.3 copy-start.8
  7.2 4.4 copy-start.4
  7.2 4.4 copy-start.3
  7.2 4.4 copy-start.2
  7.2 4.4 copy-start.1
  7.2 69.7 %all-gather.6.cloned.1.call-start = ((), (), s32[]{:S(2)}) async-start(), calls=%async_computation.2 | async-start | bytes 7077888 | tf_op jit(solution)/shard_map/all_gather | solution.py:84
  11.4 151.6 %reduce-scatter.3.cloned.1.call-start = ((), (), s32[]{:S(2)}) async-start(), calls=%async_computation.3 | async-start | bytes 7077888 | tf_op jit(solution)/shard_map/reduce_scatter | solution.py:102
  76.9 4.1 copy-start.5
  81.0 4.1 copy-start.6
  87.7 2.2 copy-start.7
  102.7 134.4 %all-gather.14.cloned.1.call-start = ((), (), s32[]{:S(2)}) async-start(), calls=%async_computation.7 | async-start | bytes 7077888 | tf_op jit(solution)/shard_map/all_gather | solution.py:121
  174.3 193.3 %reduce-scatter.5.cloned.1.call-start = ((), (), s32[]{:S(2)}) async-start(), calls=%async_computation.8 | async-start | bytes 8912896 | tf_op jit(solution)/shard_map/reduce_scatter | solution.py:128
  237.1 4.1 copy-start
  263.9 225.4 %all-gather.8.cloned.1.call-start = ((), (), s32[]{:S(2)}) async-start(), calls=%async_computation.4 | async-start | bytes 23592960 | tf_op jit(solution)/shard_map/all_gather | solution.py:113
  264.5 346.9 %all-gather.10.cloned.1.call-start = ((), (), s32[]{:S(2)}) async-start(), calls=%async_computation.5 | async-start | bytes 23592960 | tf_op jit(solution)/shard_map/all_gather | solution.py:114
  264.5 1.3 copy-start.9
  265.1 468.5 %all-gather.12.cloned.1.call-start = ((), (), s32[]{:S(2)}) async-start(), calls=%async_computation.6 | async-start | bytes 23592960 | tf_op jit(solution)/shard_map/all_gather | solution.py:115
Sparse Core Ops, SparseCore 0:
  11.5 65.3 all-gather.5
  102.9 60.0 reduce-scatter.2
  174.5 62.6 all-gather.13
  264.0 103.5 reduce-scatter.4
  369.6 119.6 all-gather.7
  491.3 119.9 all-gather.9
  613.5 119.9 all-gather.11
where the time goes:
time: 762 us
  waiting for transfers between devices  636 us (83%)
  matrix products  48.3 us (6%)
  other arithmetic  32.6 us (4%)
  local copies, waits for them, and re-layouts  29.8 us (4%)
  between operations  14.4 us (2%)
    all_gather x1, waiting for transfers between devices, per_device(): lax.all_gather(new_master, 'slot', axis=0, tiled=True)  120 us
    all_gather x1, waiting for transfers between devices, per_device(): lax.all_gather(new_b, 'slot', axis=0, tiled=True)  113 us
    all_gather x1, waiting for transfers between devices, per_device(): lax.all_gather(new_a, 'slot', axis=0, tiled=True)  112 us
    reduce_scatter x1, waiting for transfers between devices, per_device(): lax.psum_scatter(partial_value, ('slot', 'hid'), scatter_dimension=1, til...  102 us
    all_gather x1, waiting for transfers between devices, per_device(): full_weights = lax.all_gather(shard_weights, 'dp', axis=3, tiled=True)  65.2 us
    all_gather x1, waiting for transfers between devices, per_device(): next_full = lax.all_gather(next_shard, 'dp', axis=3, tiled=True)  62.7 us
    reduce_scatter x1, waiting for transfers between devices, per_device(): lax.psum_scatter(gradients.astype(jnp.bfloat16), 'dp', scatter_dimension=...  60.2 us
    gather x3, local copies, waits for them, and re-layouts, per_device(): jnp.take(state_block, wanted, axis=0)  28.7 us
  transfers between devices with their start and end apart: 7, of which 7 were waited for; matrix products, arithmetic and copies ran while one was open for 3% of the time, Pallas kernels for 0%

commit v1 on v0

--- a/solution.py
+++ b/solution.py
@@ -8,6 +8,23 @@
 beta_two = 0.95
 epsilon = 1e-08
 decay_rate = 0.1
+
+
+def laid_out(blocks, dim):
+    shape = list(blocks.shape[1:])
+    shape[dim] *= blocks.shape[0]
+    return jnp.moveaxis(blocks, 0, dim).reshape(shape)
+
+
+def gather_around(x, axis, dim):
+    size = lax.axis_size(axis)
+    ahead = [(i, (i + 1) % size) for i in range(size)]
+    blocks = [x]
+    while len(blocks) < size:
+        blocks.append(lax.ppermute(blocks[-1], axis, ahead))
+    index = lax.axis_index(axis)
+    blocks = jnp.stack(blocks)[(index - jnp.arange(size)) % size]
+    return laid_out(blocks, dim)
 
 
 def rows_by(left, right):
@@ -112,7 +129,7 @@
     gathered_states = (
         lax.all_gather(new_master, "slot", axis=0, tiled=True),
         lax.all_gather(new_a, "slot", axis=0, tiled=True),
-        lax.all_gather(new_b, "slot", axis=0, tiled=True),
+        gather_around(new_b, "slot", 0),
     )
     wanted = lax.dynamic_slice_in_dim(source, offset, local_count)
     moved_states = tuple((jnp.take(state_block, wanted, axis=0) for state_block in gathered_states))

time: 762 us -> 694 us (0.911)
  waiting for transfers between devices: 636 us -> 513 us
  local copies, waits for them, and re-layouts: 29.8 us -> 58 us
  other arithmetic: 32.6 us -> 53.4 us
    ppermute x0 -> x3, waiting for transfers between devices: none -> 277 us  [gather_around(): blocks.append(lax.ppermute(blocks[-1], axis, ahead))]
    all_gather x1, waiting for transfers between devices: 120 us -> 0.01 us  [per_device(): lax.all_gather(new_master, 'slot', axis=0, tiled=True)]
    all_gather x1 -> x0, waiting for transfers between devices: 113 us -> none  [per_device(): lax.all_gather(new_b, 'slot', axis=0, tiled=True)]
    reduce_scatter x1, waiting for transfers between devices: 102 us -> 0.01 us  [per_device(): lax.psum_scatter(partial_value, ('slot', 'hid'), scatter_dimension=1, til...]
    all_gather x1, waiting for transfers between devices: 112 us -> 46.6 us  [per_device(): lax.all_gather(new_a, 'slot', axis=0, tiled=True)]
    gather x0 -> x3, local copies, waits for them, and re-layouts: none -> 28.3 us  [gather_around(): blocks = jnp.stack(blocks)[(index - jnp.arange(size)) % size]]
    unnamed x0 -> x1, other arithmetic: none -> 15.4 us
  transfers between devices with their start and end apart: 7 -> 9, of which waited for: 7 -> 7; matrix products, arithmetic and copies ran while one was open for 3% -> 10% of each run, Pallas kernels for 0% -> 0%
where the time goes in v1:
time: 694 us
  waiting for transfers between devices  513 us (74%)
  local copies, waits for them, and re-layouts  58 us (8%)
  other arithmetic  53.4 us (8%)
  matrix products  48.3 us (7%)
  between operations  14.4 us (2%)
  starting transfers between devices  7.15 us (1%)
    ppermute x3, waiting for transfers between devices, gather_around(): blocks.append(lax.ppermute(blocks[-1], axis, ahead))  277 us
    all_gather x1, waiting for transfers between devices, per_device(): full_weights = lax.all_gather(shard_weights, 'dp', axis=3, tiled=True)  65.2 us
    all_gather x1, waiting for transfers between devices, per_device(): next_full = lax.all_gather(next_shard, 'dp', axis=3, tiled=True)  62.7 us
    reduce_scatter x1, waiting for transfers between devices, per_device(): lax.psum_scatter(gradients.astype(jnp.bfloat16), 'dp', scatter_dimension=...  60.2 us
    all_gather x1, waiting for transfers between devices, per_device(): lax.all_gather(new_a, 'slot', axis=0, tiled=True)  46.6 us
    gather x3, local copies, waits for them, and re-layouts, per_device(): jnp.take(state_block, wanted, axis=0)  28.6 us
    gather x3, local copies, waits for them, and re-layouts, gather_around(): blocks = jnp.stack(blocks)[(index - jnp.arange(size)) % size]  28.3 us
    dot_general x8, matrix products, rows_by(): lax.dot_general(left, right, (((1,), (1,)), ((), ())), preferred_element_...  21.1 us
  transfers between devices with their start and end apart: 9, of which 7 were waited for; matrix products, arithmetic and copies ran while one was open for 10% of the time, Pallas kernels for 0%

profile of v1, /device:TPU:0, one launch (start us, length us, event | category | flops | bytes accessed | tf_op | source)
XLA Modules:
  0.0 693.9 jit_solution(17376016460229325649)
XLA Ops:
  7.3 4.1 convert_element_type.49
  11.7 65.2 %all-gather.5.cloned.1.call-done = bf16[2,3,192,2048]{3,2,1,0:T(8,128)(2,1)} async-done(((bf16[2,3,192,1024]{3,2,1,0:T(8,128)(2,1)}), bf16[2,3,192,2048]{3,2,1,0:T(8,128)(2,1)}) %all-gather.5.cloned.1.call-update) | async-done | bytes 4718608 | tf_op jit(solution)/shard_map/all_gather | solution.py:101
  76.9 4.1 fusion.23
  81.0 4.0 fusion.14
  102.8 60.2 %reduce-scatter.3.cloned.1.call-done = bf16[2,3,192,1024]{3,2,1,0:T(8,128)(2,1)} async-done(((bf16[2,3,192,2048]{3,2,1,0:T(8,128)(2,1)}), bf16[2,3,192,1024]{3,2,1,0:T(8,128)(2,1)}) %reduce-scatter.3.cloned.1.call-update) | async-done | bytes 2359312 | tf_op jit(solution)/shard_map/reduce_scatter | solution.py:119
  163.0 11.4 %fusion.61 = (bf16[2,3,192,1024]{3,2,1,0:T(8,128)(2,1)}, f32[2,3,192,1024]{3,2,1,0:T(8,128)}, f32[2,3,192,1024]{3,2,1,0:T(8,128)}, f32[2,3,192,1024]{3,2,1,0:T(8,128)}) fusion(f32[2,3,192,1024]{3,2,1,0:T(8,128)} %param.14, bf16[2,3,192,1024]{3,2,1,0:T(8,128)(2,1)} %reduce-scatter.3.cloned.1.call-done, f32[2,3,192,1024]{3,2,1,0:T(8,128)} %param.15, ...), kind=kLoop, calls=%fused_computation.111 | loop fusion | flops 20054016 | bytes 33030144 | tf_op jit(solution)/shard_map/convert_element_type | solution.py:137
  174.4 62.7 %all-gather.11.cloned.1.call-done = bf16[2,3,192,2048]{3,2,1,0:T(8,128)(2,1)} async-done(((bf16[2,3,192,1024]{3,2,1,0:T(8,128)(2,1)}), bf16[2,3,192,2048]{3,2,1,0:T(8,128)(2,1)}) %all-gather.11.cloned.1.call-update) | async-done | bytes 4718608 | tf_op jit(solution)/shard_map/all_gather | solution.py:138
  237.2 4.1 fusion.20
  243.9 8.8 %fusion.17 = f32[1024,2048]{1,0:T(8,128)} fusion(bf16[1024,2048]{1,0:T(8,128)(2,1)} %param.21, bf16[2,3,192,2048]{3,2,1,0:T(8,128)(2,1)} %all-gather.11.cloned.1.call-done, f32[192,1024]{1,0:T(8,128)S(1)} %fusion.20, f32[1024]{0:T(1024)S(1)} %bitcast.83), kind=kOutput, calls=%fused_computation.40 | convolution fusion | flops 1611988992 | bytes 14946304 | tf_op jit(solution)/shard_map/dot_general | solution.py:63
  252.7 11.2 %convolution_add_fusion = f32[1024,2048]{1,0:T(8,128)} fusion(f32[1024,2048]{1,0:T(8,128)} %fusion.17, bf16[1024,2048]{1,0:T(8,128)(2,1)} %param.21, bf16[2,3,192,2048]{3,2,1,0:T(8,128)(2,1)} %all-gather.11.cloned.1.call-done, f32[192,1024]{1,0:T(8,128)S(1)} %fusion.19, f32[1024]{0:T(1024)S(1)} %bitcast.82), kind=kOutput, calls=%fused_computation.17 | convolution fusion | flops 1614086144 | bytes 23334912 | tf_op jit(solution)/shard_map/dot_general | solution.py:63
  265.1 71.5 %collective-permute-done = f32[2,3,192,1024]{3,2,1,0:T(8,128)S(1)} collective-permute-done((f32[2,3,192,1024]{3,2,1,0:T(8,128)}, f32[2,3,192,1024]{3,2,1,0:T(8,128)S(1)}, u32[]{:S(2)}, u32[]{:S(2)}) %collective-permute-start) | collective-permute-done | bytes 4718624 | tf_op jit(solution)/shard_map/ppermute | solution.py:24
  338.7 71.2 %collective-permute-done.1 = f32[2,3,192,1024]{3,2,1,0:T(8,128)S(1)} collective-permute-done((f32[2,3,192,1024]{3,2,1,0:T(8,128)S(1)}, f32[2,3,192,1024]{3,2,1,0:T(8,128)S(1)}, u32[]{:S(2)}, u32[]{:S(2)}) %collective-permute-start.1) | collective-permute-done | bytes 4718624 | tf_op jit(solution)/shard_map/ppermute | solution.py:24
  409.9 4.8 collective-permute-start.2
  415.0 134.2 %collective-permute-done.2 = f32[2,3,192,1024]{3,2,1,0:T(8,128)S(1)} collective-permute-done((f32[2,3,192,1024]{3,2,1,0:T(8,128)S(1)}, f32[2,3,192,1024]{3,2,1,0:T(8,128)S(1)}, u32[]{:S(2)}, u32[]{:S(2)}) %collective-permute-start.2) | collective-permute-done | bytes 4718624 | tf_op jit(solution)/shard_map/ppermute | solution.py:24
  549.2 5.4 pad_maximum_fusion
  554.6 11.2 %fusion.64 = (f32[4,2,3,192,512]{4,3,2,1,0:T(8,128)}, f32[4,2,3,192,512]{4,3,2,1,0:T(8,128)}) fusion(f32[4,2,3,192,1024]{4,3,2,1,0:T(8,128)S(1)} %pad_maximum_fusion), kind=kLoop, calls=%fused_computation.112 | loop fusion | bytes 37748736 | tf_op jit(solution)/shard_map/gather | solution.py:26
  565.8 8.5 %gather_fusion = f32[4,2,3,192,512]{4,3,2,1,0:T(8,128)} fusion(f32[4,2,3,192,512]{4,3,2,1,0:T(8,128)} %get-tuple-element.13, s32[1024]{0:T(1024)S(1)} %pad_clamp_fusion), kind=kCustom, calls=%fused_computation.3 | custom fusion | bytes 18874384 | tf_op jit(solution)/shard_map/gather | solution.py:26
  574.3 8.6 %gather_fusion.1 = f32[4,2,3,192,512]{4,3,2,1,0:T(8,128)} fusion(f32[4,2,3,192,512]{4,3,2,1,0:T(8,128)} %get-tuple-element.14, s32[1024]{0:T(1024)S(1)} %pad_clamp_fusion), kind=kCustom, calls=%fused_computation.4 | custom fusion | bytes 18874384 | tf_op jit(solution)/shard_map/gather | solution.py:26
  582.9 15.4 %pad_maximum_fusion.1 = f32[4,2,3,192,1024]{4,3,2,1,0:T(8,128)} fusion(f32[4,2,3,192,512]{4,3,2,1,0:T(8,128)} %gather_fusion.1, f32[4,2,3,192,512]{4,3,2,1,0:T(8,128)} %gather_fusion), kind=kLoop, calls=%fused_computation.6 | loop fusion | flops 4718592 | bytes 37748736
  598.2 9.6 %gather_fusion.4 = f32[2,3,192,1024]{3,2,1,0:T(8,128)} fusion(f32[8,3,192,1024]{3,2,1,0:T(8,128)} %bitcast.77, s32[1024]{0:T(1024)S(1)} %pad_clamp_fusion.1), kind=kCustom, calls=%fused_computation.2.clone | custom fusion | bytes 9437192 | tf_op jit(solution)/shard_map/jit(_take)/gather | solution.py:135
  609.6 9.6 %gather_fusion.2 = f32[2,3,192,1024]{3,2,1,0:T(8,128)} fusion(f32[8,3,192,1024]{3,2,1,0:T(8,128)} %all-gather.7.cloned.1.call-done, s32[1024]{0:T(1024)S(1)} %pad_clamp_fusion.1), kind=kCustom, calls=%fused_computation.clone | custom fusion | bytes 9437192 | tf_op jit(solution)/shard_map/jit(_take)/gather | solution.py:135
  619.2 46.6 %all-gather.9.cloned.1.call-done = f32[8,3,192,1024]{3,2,1,0:T(8,128)} async-done(((f32[2,3,192,1024]{3,2,1,0:T(8,128)}), f32[8,3,192,1024]{3,2,1,0:T(8,128)}) %all-gather.9.cloned.1.call-update) | async-done | bytes 18874384 | tf_op jit(solution)/shard_map/all_gather | solution.py:131
  665.8 9.4 %gather_fusion.3 = f32[2,3,192,1024]{3,2,1,0:T(8,128)} fusion(f32[8,3,192,1024]{3,2,1,0:T(8,128)} %all-gather.9.cloned.1.call-done, s32[1024]{0:T(1024)S(1)} %pad_clamp_fusion.1), kind=kCustom, calls=%fused_computation.1.clone | custom fusion | bytes 9437192 | tf_op jit(solution)/shard_map/jit(_take)/gather | solution.py:135
  675.2 11.9 %broadcast_select_fusion = (f32[2,3,192,1024]{3,2,1,0:T(8,128)}, f32[2,3,192,1024]{3,2,1,0:T(8,128)}, f32[2,3,192,1024]{3,2,1,0:T(8,128)}) fusion(f32[2,3,192,1024]{3,2,1,0:T(8,128)} %gather_fusion.4, pred[2]{0:T(512)(128)(4,1)S(1)} %get-tuple-element.11, f32[2,3,192,1024]{3,2,1,0:T(8,128)} %gather_fusion.3, f32[2,3,192,1024]{3,2,1,0:T(8,128)} %gather_fusion.2), kind=kLoop, calls=%fused_computation.32 | loop fusion | flops 3538944 | bytes 28311554 | tf_op jit(solution)/shard_map/jit(_take)/select_n | solution.py:135
  (59 shorter events, 26.0 us)
Async XLA Ops:
  7.2 4.3 copy-start.8
  7.2 4.4 copy-start.4
  7.2 4.4 copy-start.3
  7.2 4.4 copy-start.2
  7.2 4.4 copy-start.1
  7.2 69.7 %all-gather.5.cloned.1.call-start = ((), (), s32[]{:S(2)}) async-start(), calls=%async_computation.2 | async-start | bytes 7077888 | tf_op jit(solution)/shard_map/all_gather | solution.py:101
  11.4 151.6 %reduce-scatter.3.cloned.1.call-start = ((), (), s32[]{:S(2)}) async-start(), calls=%async_computation.3 | async-start | bytes 7077888 | tf_op jit(solution)/shard_map/reduce_scatter | solution.py:119
  76.9 4.1 copy-start.5
  81.0 4.1 copy-start.6
  87.7 2.2 copy-start.7
  102.8 134.4 %all-gather.11.cloned.1.call-start = ((), (), s32[]{:S(2)}) async-start(), calls=%async_computation.6 | async-start | bytes 7077888 | tf_op jit(solution)/shard_map/all_gather | solution.py:138
  174.4 433.5 %reduce-scatter.5.cloned.1.call-start = ((), (), s32[]{:S(2)}) async-start(), calls=%async_computation.7 | async-start | bytes 8912896 | tf_op jit(solution)/shard_map/reduce_scatter | solution.py:145
  237.2 4.1 copy-start
  263.9 345.7 %all-gather.7.cloned.1.call-start = ((), (), s32[]{:S(2)}) async-start(), calls=%async_computation.4 | async-start | bytes 23592960 | tf_op jit(solution)/shard_map/all_gather | solution.py:130
  263.9 150.8 %copy-start.9 = (s32[8]{0:T(128)S(1)}, s32[8]{0:T(128)}, u32[]{:S(2)}) copy-start(s32[8]{0:T(128)} %param.25) | copy-start | bytes 100
  264.5 401.3 %all-gather.9.cloned.1.call-start = ((), (), s32[]{:S(2)}) async-start(), calls=%async_computation.5 | async-start | bytes 23592960 | tf_op jit(solution)/shard_map/all_gather | solution.py:131
  265.1 71.6 %collective-permute-start = (f32[2,3,192,1024]{3,2,1,0:T(8,128)}, f32[2,3,192,1024]{3,2,1,0:T(8,128)S(1)}, u32[]{:S(2)}, u32[]{:S(2)}) collective-permute-start(f32[2,3,192,1024]{3,2,1,0:T(8,128)} %get-tuple-element.10), channel_id=1, source_target_pairs={{0,4},{4,8},{8,12},{12,0},{1,5},{5,9},{9,13},{13,1},{2,6},{6,10},{... | collective-permute-start | bytes 14155784 | tf_op jit(solution)/shard_map/ppermute | solution.py:24
  336.6 73.3 %collective-permute-start.1 = (f32[2,3,192,1024]{3,2,1,0:T(8,128)S(1)}, f32[2,3,192,1024]{3,2,1,0:T(8,128)S(1)}, u32[]{:S(2)}, u32[]{:S(2)}) collective-permute-start(f32[2,3,192,1024]{3,2,1,0:T(8,128)S(1)} %collective-permute-done), channel_id=1, source_target_pairs={{0,4},{4,8},{8,12},{12,0},{1,5},{5,9},{9,13},{13,1},{2,6},{6,10},{... | collective-permute-start | bytes 14155784 | tf_op jit(solution)/shard_map/ppermute | solution.py:24
  409.9 139.3 %collective-permute-start.2 = (f32[2,3,192,1024]{3,2,1,0:T(8,128)S(1)}, f32[2,3,192,1024]{3,2,1,0:T(8,128)S(1)}, u32[]{:S(2)}, u32[]{:S(2)}) collective-permute-start(f32[2,3,192,1024]{3,2,1,0:T(8,128)S(1)} %collective-permute-done.1), channel_id=1, source_target_pairs={{0,4},{4,8},{8,12},{12,0},{1,5},{5,9},{9,13},{13,1},{2,6},{6,10},{... | collective-permute-start | bytes 14155784 | tf_op jit(solution)/shard_map/ppermute | solution.py:24
Sparse Core Ops, SparseCore 0:
  11.5 65.3 all-gather.4
  102.9 60.0 reduce-scatter.2
  174.5 62.6 all-gather.10
  264.0 110.0 reduce-scatter.4
  376.1 167.5 all-gather.6
  545.7 119.9 all-gather.8
